TPU v7x, 256 devices: a whole 4x4x8 slice. The times are simulated.
256 devices in a mesh: section: 2 (over z_hi), dp: 16 (over z_lo, y), tensor: 8 (over x, core).
Axes of the slice: x: 4, y: 4, z: 8 (z_hi: 2, z_lo: 4; z = z_hi * 4 + z_lo), core: 2. Of those that a mesh axis runs over, the one named last changes fastest.
Arguments:
- section_input: bfloat16 [2, 1024, 8192], P('section', 'tensor', 'dp'), may hold values from -40 to 40
- norm_gain_attn: bfloat16 [2, 8192], P('section', 'dp'), may hold values from 0.099609375 to 1.8984375
- w_query: bfloat16 [2, 8192, 4096], P('section', 'dp', 'tensor'), may hold values from -0.0625 to 0.0625
- key_value_weight: bfloat16 [2, 2, 8192, 512], P('section', None, 'dp'), may hold values from -0.0625 to 0.0625
- w_output: bfloat16 [2, 4096, 8192], P('section', 'tensor', 'dp'), may hold values from -0.09375 to 0.09375
- norm_gain_ffn: bfloat16 [2, 8192], P('section', 'dp'), may hold values from 0.099609375 to 1.8984375
- w_gate_up: bfloat16 [2, 2, 8192, 14336], P('section', None, 'dp', 'tensor'), may hold values from -0.0625 to 0.0625
- w_down: bfloat16 [2, 14336, 8192], P('section', 'tensor', 'dp'), may hold values from -0.046875 to 0.046875
Outputs:
- section_output: bfloat16 [2, 1024, 8192], P('section', 'tensor', 'dp')
All inputs are finite; a program needn't handle non-finite values.
Results may differ from a plain program's by a relative error of at most 0.019.
Values may be sent and summed in bfloat16 or wider, within the bound.
A program may use at most 64 MiB of HBM per device.

v0:
```python
import math
import jax
import jax.numpy as jnp
from jax import lax
from jax.sharding import PartitionSpec as P

HEAD_SIZE = 128
QUERY_HEADS = 32
KEY_VALUE_HEADS = 4
EPS = 1e-05
THETA = 500000.0


def from_behind(x, axis, by):
    count = lax.axis_size(axis)
    return lax.ppermute(x, axis, [(i, (i + by) % count) for i in range(count)])


def apply_rotary(value_states, token_positions):
    width = value_states.shape[-1]
    half = width // 2
    freqs = jnp.exp(-(2.0 * jnp.arange(half, dtype=jnp.float32) / width) * math.log(THETA))
    angles = token_positions.astype(jnp.float32)[:, None] * freqs[None, :]
    cosine = jnp.cos(angles)[:, None, :]
    sine = jnp.sin(angles)[:, None, :]
    first = value_states[..., :half]
    second = value_states[..., half:]
    return jnp.concatenate(
        [first * cosine - second * sine, second * cosine + first * sine], axis=-1
    )


def local(
    section_input,
    norm_gain_attn,
    w_query,
    key_value_weight,
    w_output,
    norm_gain_ffn,
    w_gate_up,
    w_down,
):
    tile = section_input[0]
    rows_dev = tile.shape[0]
    cols_dev = tile.shape[1]
    tensor_count = lax.axis_size("tensor")
    data_count = lax.axis_size("dp")
    seq_total = rows_dev * tensor_count
    query_rows = seq_total // data_count
    width_total = cols_dev * data_count
    head_dim = HEAD_SIZE
    heads_dev = w_query.shape[2] // head_dim
    group_heads = QUERY_HEADS // KEY_VALUE_HEADS
    kv_dev = max(1, heads_dev // group_heads)
    per_kv = heads_dev // kv_dev
    tensor_pos = lax.axis_index("tensor")
    data_pos = lax.axis_index("dp")
    kv_first = tensor_pos * heads_dev // group_heads
    key_cols = lax.dynamic_slice_in_dim(
        key_value_weight[0], kv_first * head_dim, kv_dev * head_dim, 2
    )
    w_columns = jnp.concatenate([w_query[0], key_cols[0], key_cols[1]], axis=1)
    gain_attn = norm_gain_attn[0].astype(jnp.float32)[None, :]
    gain_ffn = norm_gain_ffn[0].astype(jnp.float32)[None, :]
    query_cols = heads_dev * head_dim
    kv_cols = kv_dev * head_dim
    query_pos = data_pos * query_rows + jnp.arange(query_rows, dtype=jnp.int32)
    all_pos = jnp.arange(seq_total, dtype=jnp.int32)
    arrived = from_behind(tile, "section", 1)
    wide = arrived.astype(jnp.float32)
    squares = lax.psum(jnp.sum(wide * wide, axis=1), "dp")
    normed_input = (wide * lax.rsqrt(squares / width_total + EPS)[:, None] * gain_attn).astype(
        jnp.bfloat16
    )
    partial_qkv = jnp.dot(
        lax.all_gather(normed_input, "tensor", axis=0, tiled=True),
        w_columns,
        preferred_element_type=jnp.float32,
    )
    query_sum = lax.psum_scatter(
        partial_qkv[:, :query_cols].astype(jnp.bfloat16), "dp", scatter_dimension=0, tiled=True
    ).astype(jnp.float32)
    key_sum = lax.psum(partial_qkv[:, query_cols:].astype(jnp.bfloat16), "dp").astype(jnp.float32)
    keys = apply_rotary(key_sum[:, :kv_cols].reshape(seq_total, kv_dev, head_dim), all_pos).astype(
        jnp.bfloat16
    )
    value_states = key_sum[:, kv_cols:].reshape(seq_total, kv_dev, head_dim).astype(jnp.bfloat16)
    query_states = apply_rotary(
        query_sum.reshape(query_rows, heads_dev, head_dim), query_pos
    ).astype(jnp.bfloat16)
    grouped = query_states.reshape(query_rows, kv_dev, per_kv, head_dim)
    scores = jnp.einsum(
        "qkgd,skd->kgqs", grouped, keys, preferred_element_type=jnp.float32
    ) * head_dim ** (-0.5)
    visible = all_pos[None, :] <= query_pos[:, None]
    weights_exp = jnp.where(visible, jnp.exp(scores), 0.0)
    probs = (weights_exp / jnp.sum(weights_exp, axis=-1, keepdims=True)).astype(jnp.bfloat16)
    mixed = (
        jnp.einsum("kgqs,skd->qkgd", probs, value_states, preferred_element_type=jnp.float32)
        .astype(jnp.bfloat16)
        .reshape(query_rows, query_cols)
    )
    attn_partial = jnp.dot(
        lax.all_gather(mixed, "dp", axis=0, tiled=True),
        w_output[0],
        preferred_element_type=jnp.float32,
    )
    attn = lax.psum_scatter(
        attn_partial.astype(jnp.bfloat16), "tensor", scatter_dimension=0, tiled=True
    ).astype(jnp.float32)
    resid = (arrived.astype(jnp.float32) + attn).astype(jnp.bfloat16)
    resid_wide = resid.astype(jnp.float32)
    squares_ffn = lax.psum(jnp.sum(resid_wide * resid_wide, axis=1), "dp")
    normed_ffn = (
        resid_wide * lax.rsqrt(squares_ffn / width_total + EPS)[:, None] * gain_ffn
    ).astype(jnp.bfloat16)
    rows_ffn = lax.all_gather(normed_ffn, "tensor", axis=0, tiled=True)
    ff_dev = w_gate_up.shape[3]
    summed = lax.psum_scatter(
        jnp.einsum("rd,gdf->rgf", rows_ffn, w_gate_up[0], preferred_element_type=jnp.float32)
        .reshape(query_rows * lax.axis_size("dp"), 2 * ff_dev)
        .astype(jnp.bfloat16),
        "dp",
        scatter_dimension=0,
        tiled=True,
    ).astype(jnp.float32)
    hidden = (jax.nn.silu(summed[:, :ff_dev]) * summed[:, ff_dev:]).astype(jnp.bfloat16)
    ffn_partial = jnp.dot(
        lax.all_gather(hidden, "dp", axis=0, tiled=True),
        w_down[0],
        preferred_element_type=jnp.float32,
    )
    ffn = lax.psum_scatter(
        ffn_partial.astype(jnp.bfloat16), "tensor", scatter_dimension=0, tiled=True
    ).astype(jnp.float32)
    result = (resid_wide + ffn).astype(jnp.bfloat16)
    return result[None]


def solution(mesh):
    placed = (
        P("section", "tensor", "dp"),
        P("section", "dp"),
        P("section", "dp", "tensor"),
        P("section", None, "dp", None),
        P("section", "tensor", "dp"),
        P("section", "dp"),
        P("section", None, "dp", "tensor"),
        P("section", "tensor", "dp"),
    )
    return jax.shard_map(
        local, mesh=mesh, in_specs=placed, out_specs=P("section", "tensor", "dp"), check_vma=False
    )
```

profile of v0, /device:TPU:8, one launch (start us, length us, event | category | flops | bytes accessed | tf_op | source)
XLA Modules:
  0.0 766.1 jit_solution(4502816704359785971)
XLA Ops:
  6.5 7.2 collective-permute-start
  13.7 0.7 mul.231
  14.4 3.1 collective-permute-done
  17.5 0.1 fusion.25
  17.6 38.6 %psum.21 = f32[128]{0:T(128)S(1)} all-reduce(f32[128]{0:T(128)S(1)} %fusion.25), channel_id=1, replica_groups=mesh['section'=2,'dp'=16,'tensor'=8] {'dp'}, use_global_device_ids=true, to_apply=%region_1.2 | all-reduce | flops 128 | bytes 1024 | tf_op jit(solution)/shard_map/psum | solution.py:71
  56.2 0.8 fusion.27
  57.0 0.0 all-gather.5.cloned.1.call-update
  57.0 0.0 all-reduce.2.cloned.1.call-start
  57.1 1.7 dynamic-slice_bitcast_fusion.1
  58.8 27.4 %all-gather.5.cloned.1.call-done = bf16[1024,512]{1,0:T(8,128)(2,1)} async-done(((bf16[128,512]{1,0:T(8,128)(2,1)}), bf16[1024,512]{1,0:T(8,128)(2,1)}) %all-gather.5.cloned.1.call-update) | async-done | bytes 1048592 | tf_op jit(solution)/shard_map/all_gather | solution.py:76
  86.2 2.4 convolution_convert_fusion.1
  88.7 0.8 slice.54
  89.5 0.0 reduce-scatter.5.cloned.1.call-start
  89.6 1.0 slice.59
  90.7 0.0 all-gather.7.cloned.1.call-start
  90.8 0.1 iota_compare_fusion
  90.9 0.2 multiply_cosine_fusion.1
  91.1 160.4 %all-reduce.2.cloned.1.call-done = bf16[1024,256]{1,0:T(8,128)(2,1)} async-done(((bf16[1024,256]{1,0:T(8,128)(2,1)}), bf16[1024,256]{1,0:T(8,128)(2,1)}) %all-reduce.2.cloned.1.call-update) | async-done | bytes 524304 | tf_op jit(solution)/shard_map/psum | solution.py:83
  251.5 1.1 fusion.33
  252.6 2.4 fusion.37
  255.0 79.3 %reduce-scatter.5.cloned.1.call-done = bf16[64,512]{1,0:T(8,128)(2,1)} async-done(((bf16[1024,512]{1,0:T(8,128)(2,1)}), bf16[64,512]{1,0:T(8,128)(2,1)}) %reduce-scatter.5.cloned.1.call-update) | async-done | bytes 65552 | tf_op jit(solution)/shard_map/reduce_scatter | solution.py:80
  334.3 0.9 reshape.220
  335.2 0.1 fusion.45
  335.4 0.6 fusion.46
  336.0 0.4 fusion.8
  336.4 0.1 copy.13
  336.4 0.6 copy.23
  337.1 0.0 reduce-scatter.7.cloned.1.call-start
  337.1 81.5 %all-gather.7.cloned.1.call-done = bf16[1024,512]{1,0:T(8,128)(2,1)} async-done(((bf16[64,512]{1,0:T(8,128)(2,1)}), bf16[1024,512]{1,0:T(8,128)(2,1)}) %all-gather.7.cloned.1.call-update) | async-done | bytes 1048592 | tf_op jit(solution)/shard_map/all_gather | solution.py:104
  418.6 3.0 convolution_convert_fusion.2
  421.7 0.0 all-gather.9.cloned.1.call-start
  421.8 33.3 %reduce-scatter.7.cloned.1.call-done = bf16[128,512]{1,0:T(8,128)(2,1)} async-done(((bf16[1024,512]{1,0:T(8,128)(2,1)}), bf16[128,512]{1,0:T(8,128)(2,1)}) %reduce-scatter.7.cloned.1.call-update) | async-done | bytes 131088 | tf_op jit(solution)/shard_map/reduce_scatter | solution.py:108
  455.1 1.0 fusion.29
  456.1 39.0 %psum.23 = f32[128]{0:T(128)S(1)} all-reduce(f32[128]{0:T(128)S(1)} %fusion.29), channel_id=1, replica_groups=mesh['section'=2,'dp'=16,'tensor'=8] {'dp'}, use_global_device_ids=true, to_apply=%region_7.8 | all-reduce | flops 128 | bytes 1024 | tf_op jit(solution)/shard_map/psum | solution.py:113
  495.1 1.7 fusion.31
  496.7 0.0 reduce-scatter.9.cloned.1.call-start
  496.8 6.0 copy.14
  502.8 18.1 %all-gather.9.cloned.1.call-done = bf16[1024,512]{1,0:T(8,128)(2,1)} async-done(((bf16[128,512]{1,0:T(8,128)(2,1)}), bf16[1024,512]{1,0:T(8,128)(2,1)}) %all-gather.9.cloned.1.call-update) | async-done | bytes 1048592 | tf_op jit(solution)/shard_map/all_gather | solution.py:117
  520.9 9.3 %convolution_convert_fusion = bf16[1024,3584]{1,0:T(8,128)(2,1)} fusion(bf16[1024,512]{1,0:T(8,128)(2,1)} %all-gather.9.cloned.1.call-done, bf16[3584,512]{1,0:T(8,128)(2,1)} %bitcast.64), kind=kOutput, calls=%fused_computation | convolution fusion | flops 3761766400 | bytes 12058624 | tf_op jit(solution)/shard_map/rd,gdf->rgf/dot_general | solution.py:120
  530.3 0.0 all-gather.11.cloned.1.call-start
  530.3 101.4 %reduce-scatter.9.cloned.1.call-done = bf16[64,3584]{1,0:T(8,128)(2,1)} async-done(((bf16[1024,3584]{1,0:T(8,128)(2,1)}), bf16[64,3584]{1,0:T(8,128)(2,1)}) %reduce-scatter.9.cloned.1.call-update) | async-done | bytes 458768 | tf_op jit(solution)/shard_map/reduce_scatter | solution.py:119
  631.7 1.1 convert_element_type.103
  632.8 0.8 fusion.24
  633.6 0.0 reduce-scatter.11.cloned.1.call-start
  633.7 85.8 %all-gather.11.cloned.1.call-done = bf16[1024,1792]{1,0:T(8,128)(2,1)} async-done(((bf16[64,1792]{1,0:T(8,128)(2,1)}), bf16[1024,1792]{1,0:T(8,128)(2,1)}) %all-gather.11.cloned.1.call-update) | async-done | bytes 3670032 | tf_op jit(solution)/shard_map/all_gather | solution.py:129
  719.4 5.1 fusion.2
  724.5 33.5 %reduce-scatter.11.cloned.1.call-done = bf16[128,512]{1,0:T(8,128)(2,1)} async-done(((bf16[1024,512]{1,0:T(8,128)(2,1)}), bf16[128,512]{1,0:T(8,128)(2,1)}) %reduce-scatter.11.cloned.1.call-update) | async-done | bytes 131088 | tf_op jit(solution)/shard_map/reduce_scatter | solution.py:133
  758.0 1.6 fusion.38
  (25 shorter events, 0.2 us)
Async XLA Ops:
  6.5 712.9 %copy-start = (bf16[1,1792,512]{2,1,0:T(8,128)(2,1)S(1)}, bf16[1,1792,512]{2,1,0:T(8,128)(2,1)}, u32[]{:S(2)}) copy-start(bf16[1,1792,512]{2,1,0:T(8,128)(2,1)} %param.15) | copy-start | bytes 5505028
  6.5 79.7 %all-gather.5.cloned.1.call-start = ((), (), s32[]{:S(2)}) async-start(), calls=%async_computation.4 | async-start | bytes 1179648 | tf_op jit(solution)/shard_map/all_gather | solution.py:76
  6.5 11.0 %collective-permute-start = (bf16[128,512]{1,0:T(8,128)(2,1)}, bf16[128,512]{1,0:T(8,128)(2,1)S(1)}, u32[]{:S(2)}, u32[]{:S(2)}) collective-permute-start(bf16[128,512]{1,0:T(8,128)(2,1)} %bitcast.70), channel_id=1, source_target_pairs={{0,128},{128,0},{1,129},{129,1},{2,130},{130,2},{3,131},{131,3},{4... | collective-permute-start | bytes 393224 | tf_op jit(solution)/shard_map/ppermute | solution.py:16
  57.0 194.5 %all-reduce.2.cloned.1.call-start = ((), (), s32[]{:S(2)}) async-start(), calls=%async_computation.5 | async-start | bytes 1048576 | tf_op jit(solution)/shard_map/psum | solution.py:83
  89.5 244.8 %reduce-scatter.5.cloned.1.call-start = ((), (), s32[]{:S(2)}) async-start(), calls=%async_computation.6 | async-start | bytes 1114112 | tf_op jit(solution)/shard_map/reduce_scatter | solution.py:80
  90.7 328.0 %all-gather.7.cloned.1.call-start = ((), (), s32[]{:S(2)}) async-start(), calls=%async_computation.7 | async-start | bytes 1114112 | tf_op jit(solution)/shard_map/all_gather | solution.py:104
  251.5 84.5 %copy-start.2 = (bf16[1024,256]{1,0:T(8,128)(2,1)S(1)}, bf16[1024,256]{1,0:T(8,128)(2,1)}, u32[]{:S(2)}) copy-start(bf16[1024,256]{1,0:T(8,128)(2,1)} %all-reduce.2.cloned.1.call-done) | copy-start | bytes 1572868
  336.3 85.4 %copy-start.3 = (bf16[1,512]{1,0:T(2,128)(2,1)S(1)}, bf16[1,512]{1,0:T(2,128)(2,1)}, u32[]{:S(2)}) copy-start(bf16[1,512]{1,0:T(2,128)(2,1)} %param.13) | copy-start | bytes 3076
  337.1 118.0 %reduce-scatter.7.cloned.1.call-start = ((), (), s32[]{:S(2)}) async-start(), calls=%async_computation.8 | async-start | bytes 1179648 | tf_op jit(solution)/shard_map/reduce_scatter | solution.py:108
  421.7 99.2 %all-gather.9.cloned.1.call-start = ((), (), s32[]{:S(2)}) async-start(), calls=%async_computation.9 | async-start | bytes 1179648 | tf_op jit(solution)/shard_map/all_gather | solution.py:117
  496.7 134.9 %reduce-scatter.9.cloned.1.call-start = ((), (), s32[]{:S(2)}) async-start(), calls=%async_computation.10 | async-start | bytes 7798784 | tf_op jit(solution)/shard_map/reduce_scatter | solution.py:119
  530.3 189.1 %all-gather.11.cloned.1.call-start = ((), (), s32[]{:S(2)}) async-start(), calls=%async_computation.11 | async-start | bytes 3899392 | tf_op jit(solution)/shard_map/all_gather | solution.py:129
  633.6 124.4 %copy-start.1 = (bf16[128,512]{1,0:T(8,128)(2,1)S(1)}, bf16[128,512]{1,0:T(8,128)(2,1)}, u32[]{:S(2)}) copy-start(bf16[128,512]{1,0:T(8,128)(2,1)} %reduce-scatter.7.cloned.1.call-done) | copy-start | bytes 393220
  633.6 124.4 %reduce-scatter.11.cloned.1.call-start = ((), (), s32[]{:S(2)}) async-start(), calls=%async_computation.12 | async-start | bytes 1179648 | tf_op jit(solution)/shard_map/reduce_scatter | solution.py:133
Sparse Core Ops, SparseCore 0:
  57.2 29.0 all-gather.4
  89.7 161.8 all-reduce.1
  254.0 80.2 reduce-scatter.4
  337.2 81.3 all-gather.6
  421.8 33.1 reduce-scatter.6
  496.9 24.0 all-gather.8
  530.4 101.2 reduce-scatter.8
  633.7 85.6 all-gather.10
  724.7 33.2 reduce-scatter.10
where the time goes:
time: 767 us; the launch traced here: 766 us
  waiting for transfers between devices  624 us (81%)
  blocking collectives  77.6 us (10%)
  matrix products  20.8 us (3%)
  between operations  13.4 us (2%)
  other arithmetic  11.6 us (2%)
  local copies, waits for them, and re-layouts  11.3 us (1%)
    psum x1, waiting for transfers between devices, local(): lax.psum(partial_qkv[:, query_cols:].astype(jnp.bfloat16), 'dp')  160 us
    reduce_scatter x1, waiting for transfers between devices, local(): lax.psum_scatter(jnp.einsum('rd,gdf->rgf', rows_ffn, w_gate_up[0], prefer...  101 us
    all_gather x1, waiting for transfers between devices, local(): lax.all_gather(hidden, 'dp', axis=0, tiled=True)  85.8 us
    all_gather x1, waiting for transfers between devices, local(): lax.all_gather(mixed, 'dp', axis=0, tiled=True)  81.5 us
    reduce_scatter x1, waiting for transfers between devices, local(): lax.psum_scatter(partial_qkv[:, :query_cols].astype(jnp.bfloat16), 'dp',...  79.3 us
    psum x1, blocking collectives, local(): squares_ffn = lax.psum(jnp.sum(resid_wide * resid_wide, axis=1), 'dp')  39 us
    psum x1, blocking collectives, local(): squares = lax.psum(jnp.sum(wide * wide, axis=1), 'dp')  38.6 us
    reduce_scatter x1, waiting for transfers between devices, local(): lax.psum_scatter(ffn_partial.astype(jnp.bfloat16), 'tensor', scatter_dime...  33.5 us
  transfers between devices with their start and end apart: 10, of which 10 were waited for; matrix products, arithmetic and copies ran while one was open for 2% of the time, Pallas kernels for 0%

commit v1 on v0

--- a/solution.py
+++ b/solution.py
@@ -9,6 +9,28 @@
 KEY_VALUE_HEADS = 4
 EPS = 1e-05
 THETA = 500000.0
+
+
+def joined_along(blocks, dim):
+    blocks = jnp.moveaxis(blocks, 0, dim)
+    shape = blocks.shape
+    return blocks.reshape(*shape[:dim], shape[dim] * shape[dim + 1], *shape[dim + 2 :])
+
+
+def gather_around(x, axis, dim):
+    size = lax.axis_size(axis)
+    pairs = [(i, (i + 1) % size) for i in range(size)]
+    back = [(b, a) for a, b in pairs]
+    lower, upper = ([], [])
+    for hop in range(size - 1):
+        if hop % 2 == 0:
+            lower.append(lax.ppermute(lower[-1] if lower else x, axis, pairs))
+        else:
+            upper.append(lax.ppermute(upper[-1] if upper else x, axis, back))
+    parts = jnp.stack([*lower[::-1], x, *upper])
+    shift = lax.axis_index(axis) - len(lower)
+    parts = parts[(jnp.arange(size) - shift) % size]
+    return joined_along(parts, dim)
 
 
 def from_behind(x, axis, by):
@@ -73,9 +95,7 @@
         jnp.bfloat16
     )
     partial_qkv = jnp.dot(
-        lax.all_gather(normed_input, "tensor", axis=0, tiled=True),
-        w_columns,
-        preferred_element_type=jnp.float32,
+        gather_around(normed_input, "tensor", 0), w_columns, preferred_element_type=jnp.float32
     )
     query_sum = lax.psum_scatter(
         partial_qkv[:, :query_cols].astype(jnp.bfloat16), "dp", scatter_dimension=0, tiled=True

time: 767 us -> 767 us (level)
  waiting for transfers between devices: 624 us -> 612 us
  starting transfers between devices: 7.53 us -> 16.4 us
    all_gather x1 -> x0, waiting for transfers between devices: 27.4 us -> none  [local(): lax.all_gather(normed_input, 'tensor', axis=0, tiled=True)]
    ppermute x0 -> x7, waiting for transfers between devices: none -> 11.9 us  [the longest x4 11.9 us: gather_around(): lower.append(lax.ppermute(lower[-1] if lower else x, axis, pairs))]
    ppermute x0 -> x7, starting transfers between devices: none -> 8.87 us  [the longest x3 8.84 us: gather_around(): upper.append(lax.ppermute(upper[-1] if upper else x, axis, back))]
  transfers between devices with their start and end apart: 10 -> 16, of which waited for: 10 -> 13; matrix products, arithmetic and copies ran while one was open for 2% -> 2% of each run, Pallas kernels for 0% -> 0%
where the time goes in v1:
time: 767 us; the launch traced here: 766 us
  waiting for transfers between devices  612 us (80%)
  blocking collectives  77.6 us (10%)
  matrix products  20.8 us (3%)
  starting transfers between devices  16.4 us (2%)
  local copies, waits for them, and re-layouts  14.7 us (2%)
  between operations  13.8 us (2%)
  other arithmetic  11.1 us (1%)
    psum x1, waiting for transfers between devices, local(): lax.psum(partial_qkv[:, query_cols:].astype(jnp.bfloat16), 'dp')  164 us
    reduce_scatter x1, waiting for transfers between devices, local(): lax.psum_scatter(jnp.einsum('rd,gdf->rgf', rows_ffn, w_gate_up[0], prefer...  102 us
    all_gather x1, waiting for transfers between devices, local(): lax.all_gather(hidden, 'dp', axis=0, tiled=True)  85.4 us
    all_gather x1, waiting for transfers between devices, local(): lax.all_gather(mixed, 'dp', axis=0, tiled=True)  81.5 us
    reduce_scatter x1, waiting for transfers between devices, local(): lax.psum_scatter(partial_qkv[:, :query_cols].astype(jnp.bfloat16), 'dp',...  79.3 us
    psum x1, blocking collectives, local(): squares_ffn = lax.psum(jnp.sum(resid_wide * resid_wide, axis=1), 'dp')  39 us
    psum x1, blocking collectives, local(): squares = lax.psum(jnp.sum(wide * wide, axis=1), 'dp')  38.6 us
    reduce_scatter x1, waiting for transfers between devices, local(): lax.psum_scatter(ffn_partial.astype(jnp.bfloat16), 'tensor', scatter_dime...  33.4 us
  transfers between devices with their start and end apart: 16, of which 13 were waited for; matrix products, arithmetic and copies ran while one was open for 2% of the time, Pallas kernels for 0%

profile of v1, /device:TPU:8, one launch (start us, length us, event | category | flops | bytes accessed | tf_op | source)
XLA Modules:
  0.0 766.1 jit_solution(2201508431720787685)
XLA Ops:
  6.5 7.2 collective-permute-start
  13.7 0.7 mul.231
  14.4 3.1 collective-permute-done
  17.5 0.1 fusion.25
  17.6 38.6 %psum.21 = f32[128]{0:T(128)S(1)} all-reduce(f32[128]{0:T(128)S(1)} %fusion.25), channel_id=1, replica_groups=mesh['section'=2,'dp'=16,'tensor'=8] {'dp'}, use_global_device_ids=true, to_apply=%region_1.2 | all-reduce | flops 128 | bytes 1024 | tf_op jit(solution)/shard_map/psum | solution.py:93
  56.2 0.1 fusion.27
  56.4 5.6 collective-permute-done.1
  62.0 3.0 collective-permute-start.5
  64.9 2.6 collective-permute-done.2
  67.6 3.0 collective-permute-start.6
  70.6 2.6 collective-permute-done.3
  73.2 1.7 dynamic-slice_bitcast_fusion.1
  74.9 2.9 collective-permute-start.7
  77.8 1.1 collective-permute-done.4
  78.9 0.9 bitcast_dynamic-update-slice_fusion.7
  79.9 0.1 bitcast_dynamic-update-slice_fusion.3
  80.0 0.9 bitcast_dynamic-update-slice_fusion.1
  80.9 1.6 gather_fusion
  82.5 2.4 convolution_convert_fusion.1
  85.0 0.8 slice.56
  85.9 1.1 slice.61
  87.1 0.1 iota_compare_fusion
  87.2 0.2 multiply_cosine_fusion.1
  87.4 163.7 %all-reduce.2.cloned.1.call-done = bf16[1024,256]{1,0:T(8,128)(2,1)} async-done(((bf16[1024,256]{1,0:T(8,128)(2,1)}), bf16[1024,256]{1,0:T(8,128)(2,1)}) %all-reduce.2.cloned.1.call-update) | async-done | bytes 524304 | tf_op jit(solution)/shard_map/psum | solution.py:103
  251.1 1.1 fusion.33
  252.2 2.4 fusion.37
  254.6 79.3 %reduce-scatter.5.cloned.1.call-done = bf16[64,512]{1,0:T(8,128)(2,1)} async-done(((bf16[1024,512]{1,0:T(8,128)(2,1)}), bf16[64,512]{1,0:T(8,128)(2,1)}) %reduce-scatter.5.cloned.1.call-update) | async-done | bytes 65552 | tf_op jit(solution)/shard_map/reduce_scatter | solution.py:100
  333.9 0.9 reshape.273
  334.8 0.1 fusion.47
  335.0 0.6 fusion.48
  335.6 0.4 fusion.8
  336.0 0.6 copy.23
  336.7 81.5 %all-gather.4.cloned.1.call-done = bf16[1024,512]{1,0:T(8,128)(2,1)} async-done(((bf16[64,512]{1,0:T(8,128)(2,1)}), bf16[1024,512]{1,0:T(8,128)(2,1)}) %all-gather.4.cloned.1.call-update) | async-done | bytes 1048592 | tf_op jit(solution)/shard_map/all_gather | solution.py:124
  418.2 3.0 convolution_convert_fusion.2
  421.4 33.3 %reduce-scatter.7.cloned.1.call-done = bf16[128,512]{1,0:T(8,128)(2,1)} async-done(((bf16[1024,512]{1,0:T(8,128)(2,1)}), bf16[128,512]{1,0:T(8,128)(2,1)}) %reduce-scatter.7.cloned.1.call-update) | async-done | bytes 131088 | tf_op jit(solution)/shard_map/reduce_scatter | solution.py:128
  454.7 1.0 fusion.29
  455.7 39.0 %psum.23 = f32[128]{0:T(128)S(1)} all-reduce(f32[128]{0:T(128)S(1)} %fusion.29), channel_id=1, replica_groups=mesh['section'=2,'dp'=16,'tensor'=8] {'dp'}, use_global_device_ids=true, to_apply=%region_7.8 | all-reduce | flops 128 | bytes 1024 | tf_op jit(solution)/shard_map/psum | solution.py:133
  494.7 1.7 fusion.31
  496.5 6.0 copy.14
  502.4 18.1 %all-gather.6.cloned.1.call-done = bf16[1024,512]{1,0:T(8,128)(2,1)} async-done(((bf16[128,512]{1,0:T(8,128)(2,1)}), bf16[1024,512]{1,0:T(8,128)(2,1)}) %all-gather.6.cloned.1.call-update) | async-done | bytes 1048592 | tf_op jit(solution)/shard_map/all_gather | solution.py:137
  520.5 9.3 %convolution_convert_fusion = bf16[1024,3584]{1,0:T(8,128)(2,1)} fusion(bf16[1024,512]{1,0:T(8,128)(2,1)} %all-gather.6.cloned.1.call-done, bf16[3584,512]{1,0:T(8,128)(2,1)} %bitcast.83), kind=kOutput, calls=%fused_computation.1 | convolution fusion | flops 3761766400 | bytes 12058624 | tf_op jit(solution)/shard_map/rd,gdf->rgf/dot_general | solution.py:140
  529.9 101.8 %reduce-scatter.9.cloned.1.call-done = bf16[64,3584]{1,0:T(8,128)(2,1)} async-done(((bf16[1024,3584]{1,0:T(8,128)(2,1)}), bf16[64,3584]{1,0:T(8,128)(2,1)}) %reduce-scatter.9.cloned.1.call-update) | async-done | bytes 458768 | tf_op jit(solution)/shard_map/reduce_scatter | solution.py:139
  631.8 1.1 convert_element_type.103
  632.8 0.8 fusion.24
  633.8 85.4 %all-gather.8.cloned.1.call-done = bf16[1024,1792]{1,0:T(8,128)(2,1)} async-done(((bf16[64,1792]{1,0:T(8,128)(2,1)}), bf16[1024,1792]{1,0:T(8,128)(2,1)}) %all-gather.8.cloned.1.call-update) | async-done | bytes 3670032 | tf_op jit(solution)/shard_map/all_gather | solution.py:149
  719.1 5.1 fusion.2
  724.2 33.4 %reduce-scatter.11.cloned.1.call-done = bf16[128,512]{1,0:T(8,128)(2,1)} async-done(((bf16[1024,512]{1,0:T(8,128)(2,1)}), bf16[128,512]{1,0:T(8,128)(2,1)}) %reduce-scatter.11.cloned.1.call-update) | async-done | bytes 131088 | tf_op jit(solution)/shard_map/reduce_scatter | solution.py:153
  757.6 1.6 fusion.38
  (47 shorter events, 0.7 us)
Async XLA Ops:
  6.5 712.6 %copy-start = (bf16[1,1792,512]{2,1,0:T(8,128)(2,1)S(1)}, bf16[1,1792,512]{2,1,0:T(8,128)(2,1)}, u32[]{:S(2)}) copy-start(bf16[1,1792,512]{2,1,0:T(8,128)(2,1)} %param.15) | copy-start | bytes 5505028
  6.5 244.6 %all-reduce.2.cloned.1.call-start = ((), (), s32[]{:S(2)}) async-start(), calls=%async_computation.4 | async-start | bytes 1048576 | tf_op jit(solution)/shard_map/psum | solution.py:103
  6.5 11.0 %collective-permute-start = (bf16[128,512]{1,0:T(8,128)(2,1)}, bf16[128,512]{1,0:T(8,128)(2,1)S(1)}, u32[]{:S(2)}, u32[]{:S(2)}) collective-permute-start(bf16[128,512]{1,0:T(8,128)(2,1)} %bitcast.91), channel_id=1, source_target_pairs={{0,128},{128,0},{1,129},{129,1},{2,130},{130,2},{3,131},{131,3},{4... | collective-permute-start | bytes 393224 | tf_op jit(solution)/shard_map/ppermute | solution.py:38
  56.4 5.6 collective-permute-start.1
  62.0 5.6 collective-permute-start.2
  62.0 5.6 collective-permute-start.5
  67.6 5.6 collective-permute-start.3
  67.6 7.3 collective-permute-start.6
  73.2 5.7 collective-permute-start.4
  74.9 6.0 collective-permute-start.7
  85.8 248.1 %reduce-scatter.5.cloned.1.call-start = ((), (), s32[]{:S(2)}) async-start(), calls=%async_computation.5 | async-start | bytes 1114112 | tf_op jit(solution)/shard_map/reduce_scatter | solution.py:100
  87.0 331.3 %all-gather.4.cloned.1.call-start = ((), (), s32[]{:S(2)}) async-start(), calls=%async_computation.6 | async-start | bytes 1114112 | tf_op jit(solution)/shard_map/all_gather | solution.py:124
  251.1 84.5 %copy-start.2 = (bf16[1024,256]{1,0:T(8,128)(2,1)S(1)}, bf16[1024,256]{1,0:T(8,128)(2,1)}, u32[]{:S(2)}) copy-start(bf16[1024,256]{1,0:T(8,128)(2,1)} %all-reduce.2.cloned.1.call-done) | copy-start | bytes 1572868
  335.9 85.4 %copy-start.3 = (bf16[1,512]{1,0:T(2,128)(2,1)S(1)}, bf16[1,512]{1,0:T(2,128)(2,1)}, u32[]{:S(2)}) copy-start(bf16[1,512]{1,0:T(2,128)(2,1)} %param.13) | copy-start | bytes 3076
  336.7 118.0 %reduce-scatter.7.cloned.1.call-start = ((), (), s32[]{:S(2)}) async-start(), calls=%async_computation.7 | async-start | bytes 1179648 | tf_op jit(solution)/shard_map/reduce_scatter | solution.py:128
  421.3 99.2 %all-gather.6.cloned.1.call-start = ((), (), s32[]{:S(2)}) async-start(), calls=%async_computation.8 | async-start | bytes 1179648 | tf_op jit(solution)/shard_map/all_gather | solution.py:137
  496.4 135.3 %reduce-scatter.9.cloned.1.call-start = ((), (), s32[]{:S(2)}) async-start(), calls=%async_computation.9 | async-start | bytes 7798784 | tf_op jit(solution)/shard_map/reduce_scatter | solution.py:139
  529.9 189.3 %all-gather.8.cloned.1.call-start = ((), (), s32[]{:S(2)}) async-start(), calls=%async_computation.10 | async-start | bytes 3899392 | tf_op jit(solution)/shard_map/all_gather | solution.py:149
  633.7 123.9 %copy-start.1 = (bf16[128,512]{1,0:T(8,128)(2,1)S(1)}, bf16[128,512]{1,0:T(8,128)(2,1)}, u32[]{:S(2)}) copy-start(bf16[128,512]{1,0:T(8,128)(2,1)} %reduce-scatter.7.cloned.1.call-done) | copy-start | bytes 393220
  633.7 123.9 %reduce-scatter.11.cloned.1.call-start = ((), (), s32[]{:S(2)}) async-start(), calls=%async_computation.11 | async-start | bytes 1179648 | tf_op jit(solution)/shard_map/reduce_scatter | solution.py:153
Sparse Core Ops, SparseCore 0:
  86.0 165.1 all-reduce.1
  253.6 80.2 reduce-scatter.4
  336.8 81.3 all-gather.3
  421.4 33.1 reduce-scatter.6
  496.5 23.9 all-gather.5
  530.0 101.7 reduce-scatter.8
  633.8 85.2 all-gather.7
  724.4 33.1 reduce-scatter.10
